TPU v7x, 256 devices: a whole 4x4x8 slice. The times are simulated.
256 devices in a mesh: row: 16 (over x, y_hi, core), col: 16 (over z, y_lo).
Axes of the slice: x: 4, y: 4 (y_hi: 2, y_lo: 2; y = y_hi * 2 + y_lo), z: 8, core: 2. Of those that a mesh axis runs over, the one named last changes fastest.
Arguments:
- positions: float32 [3, 16384], P(None, ('row', 'col')), may hold values from -0.2 to 63.2, as said below
- radii: float32 [16384], P(('row', 'col')), may hold values from 0.1 to 0.28
- basis: float32 [32, 3, 16384], P(None, None, ('row', 'col')), may hold values from -0.0112763724 to 0.0112763724, as said below
- rhs: float32 [3, 16384], P(None, ('row', 'col')), may hold values from -6 to 6
Outputs:
- solution: float32 [3, 16384], P(None, ('row', 'col'))
- residual: float32 [3, 16384], P(None, ('row', 'col'))
Inputs may be any that keep to these rules, and one draw needn't show every extreme that they name: `positions`: every coordinate lies within 0.2 of a whole number and any two centres are 0.6 or more apart, more than the sum of any two radii. `basis`: the 32 vectors are linearly independent.
All inputs are finite; a program needn't handle non-finite values.
Results may differ from a plain program's by a relative error of at most 0.0003.
Values sent between devices are 32-bit elements; how exact they have to be, the bound alone decides.
A program may use at most 64 MiB of HBM per device.

v0:
```python
import math
import jax
import jax.numpy as jnp
from jax import lax
from jax.sharding import PartitionSpec as P

ITERS = 2
far_scale = 1.0 / (8.0 * math.pi)
self_scale = 1.0 / (6.0 * math.pi)
highest = lax.Precision.HIGHEST


def contract(left, right):
    return lax.dot_general(
        left, right, (((1,), (1,)), ((), ())), precision=highest, preferred_element_type=jnp.float32
    )


def block_apply(out_pos, out_rad, out_index, in_pos, in_rad, in_index, fields):
    deltas = [out_pos[axis_id][:, None] - in_pos[axis_id][None, :] for axis_id in range(3)]
    coincide = out_index[:, None] == in_index[None, :]
    dist_sq = deltas[0] * deltas[0] + deltas[1] * deltas[1] + deltas[2] * deltas[2]
    safe_sq = jnp.where(coincide, jnp.ones_like(dist_sq), dist_sq)
    inv_sq = 1.0 / safe_sq
    inv_dist = jnp.sqrt(inv_sq)
    radius_sum = (out_rad * out_rad)[:, None] + (in_rad * in_rad)[None, :]
    scaled = far_scale * inv_dist
    isotropic = scaled * (1.0 + radius_sum * inv_sq / 3.0)
    own_term = jnp.broadcast_to((self_scale / out_rad)[:, None], isotropic.shape)
    isotropic = jnp.where(coincide, own_term, isotropic)
    along = jnp.where(
        coincide, jnp.zeros_like(dist_sq), scaled * (1.0 - radius_sum * inv_sq) * inv_sq
    )
    tensors = {}
    for first in range(3):
        for second in range(first, 3):
            entry = along * deltas[first] * deltas[second]
            if first == second:
                entry = entry + isotropic
            tensors[first, second] = entry
    results = []
    for first in range(3):
        total = None
        for second in range(3):
            term = contract(fields[:, second, :], tensors[min(first, second), max(first, second)])
            total = term if total is None else total + term
        results.append(total)
    return jnp.stack(results, axis=1)


def field_apply(out_pos, out_rad, out_index, in_pos, in_rad, in_index, fields, width):
    count = out_rad.shape[0] // width
    pos_blocks = out_pos.reshape(3, count, width).transpose(1, 0, 2)
    rad_blocks = out_rad.reshape(count, width)
    index_blocks = out_index.reshape(count, width)

    def one_block(packed):
        return block_apply(packed[0], packed[1], packed[2], in_pos, in_rad, in_index, fields)

    stacked = lax.map(one_block, (pos_blocks, rad_blocks, index_blocks))
    return stacked.transpose(1, 2, 0, 3).reshape(fields.shape[0], 3, count * width)


def body(positions, radii, basis, rhs):
    cols_count = lax.axis_size("col")
    row_id = lax.axis_index("row")
    col_id = lax.axis_index("col")
    width = positions.shape[1]
    vectors_count = basis.shape[0]
    target_pos, target_rad = (
        lax.all_gather(positions, "row", axis=1, tiled=True),
        lax.all_gather(radii, "row", axis=0, tiled=True),
    )
    source_pos, source_rad = (
        lax.all_gather(positions, "col", axis=1, tiled=True),
        lax.all_gather(radii, "col", axis=0, tiled=True),
    )
    target_span = target_rad.shape[0]
    source_span = source_rad.shape[0]
    target_order = jnp.arange(target_span, dtype=jnp.int32)
    target_index = (target_order // width * cols_count + col_id) * width + target_order % width
    source_index = row_id * (cols_count * width) + jnp.arange(source_span, dtype=jnp.int32)

    def fold_sources(carry, piece):
        count = piece.shape[2]
        in_pos = lax.slice_in_dim(source_pos, 0, count, axis=1)
        in_rad = lax.slice_in_dim(source_rad, 0, count, axis=0)
        in_index = lax.slice_in_dim(source_index, 0, count, axis=0)
        return carry + field_apply(
            target_pos, target_rad, target_index, in_pos, in_rad, in_index, piece, width
        )

    empty_rows = jnp.zeros((vectors_count, 3, target_span), jnp.float32)
    partial_basis = fold_sources(
        empty_rows, jax.tree.map(lambda a: lax.all_gather(a, "col", axis=2, tiled=True), basis)
    )
    basis_image = lax.psum_scatter(partial_basis, "row", scatter_dimension=2, tiled=True)
    gram_part = jnp.einsum("kcp,lcp->kl", basis, basis_image, precision=highest)
    load_part = jnp.einsum("kcp,cp->k", basis, rhs, precision=highest)
    gram, load = lax.psum((gram_part, load_part), ("row", "col"))
    factor = jnp.linalg.cholesky(gram)

    def coarse_solve(vector):
        return jax.scipy.linalg.cho_solve((factor, True), vector)

    def combine(weights, fields):
        return jnp.einsum("k,kcp->cp", weights, fields, precision=highest)

    def correlation_of(field):
        return jnp.einsum("kcp,cp->k", basis_image, field, precision=highest)

    coarse = coarse_solve(load)
    solution = combine(coarse, basis)
    residual = rhs - combine(coarse, basis_image)

    def residual_stats(field):
        return lax.psum((correlation_of(field), jnp.sum(field * field)), ("row", "col"))

    correlation, norm_now = residual_stats(residual)
    projection = coarse_solve(correlation)
    direction = residual - combine(projection, basis)
    for iteration in range(ITERS):
        empty = jnp.zeros((1, 3, target_span), jnp.float32)
        partial_image = fold_sources(
            empty,
            jax.tree.map(lambda a: lax.all_gather(a, "col", axis=2, tiled=True), direction[None]),
        )
        image = lax.psum_scatter(partial_image, "row", scatter_dimension=2, tiled=True)[0]
        curvature = lax.psum(jnp.sum(direction * image), ("row", "col"))
        step_size = norm_now / curvature
        solution = solution + step_size * direction
        residual = residual - step_size * image
        if iteration + 1 < ITERS:
            correlation, norm_next = residual_stats(residual)
            projection = coarse_solve(correlation)
            direction = residual + norm_next / norm_now * direction - combine(projection, basis)
            norm_now = norm_next
    return (solution, residual)


def solution(mesh):
    return jax.shard_map(
        body,
        mesh=mesh,
        in_specs=(
            P(None, ("row", "col")),
            P(("row", "col")),
            P(None, None, ("row", "col")),
            P(None, ("row", "col")),
        ),
        out_specs=(P(None, ("row", "col")), P(None, ("row", "col"))),
        check_vma=False,
    )
```

profile of v0, /device:TPU:1, one launch (start us, length us, event | category | flops | bytes accessed | tf_op | source)
XLA Modules:
  0.0 1161.8 jit_solution(4575639744863065165)
XLA Ops:
  7.2 26.0 %all-gather.2 = f32[16,64,3]{1,2,0:T(4,128)S(1)} all-gather(f32[1,64,3]{1,2,0:T(4,128)} %bitcast.659), channel_id=1, replica_groups=mesh['row'=16,'col'=16] {'row'}, dimensions={0}, use_global_device_ids=true | all-gather | bytes 13056 | tf_op jit(solution)/shard_map/all_gather | solution.py:71
  33.2 28.7 %all-gather.3 = f32[16,64,3]{1,2,0:T(4,128)S(1)} all-gather(f32[1,64,3]{1,2,0:T(4,128)} %bitcast.660), channel_id=1, replica_groups=mesh['row'=16,'col'=16] {'col'}, dimensions={0}, use_global_device_ids=true | all-gather | bytes 13056 | tf_op jit(solution)/shard_map/all_gather | solution.py:75
  61.8 1.3 dynamic-slice
  63.8 0.9 dynamic-update-slice.3
  64.6 39.9 %all-reduce = f32[1024]{0:T(1024)S(1)} all-reduce(f32[1024]{0:T(1024)S(1)} %dynamic-update-slice.3), channel_id=1, replica_groups=mesh['row'=16,'col'=16] {'row'}, use_global_device_ids=true, to_apply=%add | all-reduce | flops 1024 | bytes 8192
  104.6 1.3 dynamic-slice.1
  106.5 0.9 dynamic-update-slice.4
  107.4 23.7 %all-reduce.1 = f32[1024]{0:T(1024)S(1)} all-reduce(f32[1024]{0:T(1024)S(1)} %dynamic-update-slice.4), channel_id=1, replica_groups=mesh['row'=16,'col'=16] {'col'}, use_global_device_ids=true, to_apply=%add.1 | all-reduce | flops 1024 | bytes 8192
  131.4 0.9 copy.39
  132.3 49.4 %all_gather.25 = f32[32,3,1024]{0,1,2:T(4,128)S(1)} all-gather(f32[32,3,64]{0,1,2:T(4,128)S(1)} %copy.39), channel_id=1, replica_groups=mesh['row'=16,'col'=16] {'col'}, dimensions={2}, use_global_device_ids=true | all-gather | bytes 417792 | tf_op jit(solution)/shard_map/all_gather | solution.py:95
  181.7 0.8 copy.41
  182.6 103.6 %while.39 = (s32[]{:T(128)}, f32[16,32,3,64]{3,1,2,0:T(8,128)S(1)}, s32[16,64]{1,0:T(8,128)S(1)}, f32[16,3,64]{2,1,0:T(4,128)S(1)}, f32[3,1024]{1,0:T(4,128)S(1)...) while((s32[]{:T(128)}, f32[16,32,3,64]{3,1,2,0:T(8,128)S(1)}, ...), condition=%wide.region_1.2_spmd.clone, body=%wide.region_0.1_spmd.clone.sunk | while | flops 239297664 | bytes 2417017 | solution.py:60
  183.0 0.7 fusion.370
  185.6 0.7 convolution_add_fusion.10
  189.4 0.7 fusion.370
  192.1 0.7 convolution_add_fusion.10
  195.9 0.7 fusion.370
  198.6 0.7 convolution_add_fusion.10
  202.4 0.7 fusion.370
  205.1 0.7 convolution_add_fusion.10
  208.9 0.7 fusion.370
  211.6 0.7 convolution_add_fusion.10
  215.4 0.7 fusion.370
  218.0 0.7 convolution_add_fusion.10
  221.8 0.7 fusion.370
  224.5 0.7 convolution_add_fusion.10
  228.3 0.7 fusion.370
  231.0 0.7 convolution_add_fusion.10
  234.8 0.7 fusion.370
  237.5 0.7 convolution_add_fusion.10
  241.3 0.7 fusion.370
  243.9 0.7 convolution_add_fusion.10
  247.7 0.7 fusion.370
  250.4 0.7 convolution_add_fusion.10
  254.2 0.7 fusion.370
  256.9 0.7 convolution_add_fusion.10
  260.7 0.7 fusion.370
  267.2 0.7 fusion.370
  273.7 0.7 fusion.370
  280.1 0.7 fusion.370
  282.8 0.7 convolution_add_fusion.10
  286.2 0.9 copy.64
  287.2 1.5 reshape.352
  288.9 75.8 %reduce-scatter.10.cloned.1.call-done = f32[64,96]{1,0:T(8,128)} async-done(((f32[1024,96]{1,0:T(8,128)}), f32[64,96]{1,0:T(8,128)}) %reduce-scatter.10.cloned.1.call-update) | async-done | bytes 24592
  364.8 0.9 reshape.353
  366.0 77.7 %all-reduce.4 = (f32[32,32]{0,1:T(8,128)S(1)}, f32[32]{0:T(128)S(1)}) all-reduce(f32[32,32]{0,1:T(8,128)S(1)} %convolution_bitcast_fusion.18, f32[32]{0:T(128)S(1)} %convolution_bitcast_fusion.27), channel_id=1, replica_groups=mesh['row'=16,'col'=16] {'row','col'}, use_global_device_ids=true, to_apply=%region_3.4 | all-reduce | flops 1056 | bytes 8448 | tf_op jit(solution)/shard_map/psum | solution.py:100
  443.7 2.9 cholesky.18
  447.9 2.4 custom-call.10
  451.6 73.1 %psum.59 = f32[32]{0:T(128)S(1)} all-reduce(f32[32]{0:T(128)S(1)} %convolution_bitcast_fusion.26), channel_id=1, replica_groups=mesh['row'=16,'col'=16] {'row','col'}, use_global_device_ids=true, to_apply=%region_9.11 | all-reduce | flops 32 | bytes 256 | tf_op jit(solution)/shard_map/psum | solution.py:117
  525.1 24.3 %all-gather.4 = f32[16,64,3]{1,2,0:T(4,128)S(1)} all-gather(f32[1,64,3]{1,2,0:T(4,128)S(1)} %bitcast.652), channel_id=2, replica_groups=mesh['row'=16,'col'=16] {'col'}, dimensions={0}, use_global_device_ids=true | all-gather | bytes 13056 | tf_op jit(solution)/shard_map/all_gather | solution.py:126
  549.6 95.1 %while.40 = (s32[]{:T(128)}, f32[16,1,3,64]{3,2,1,0:T(4,128)S(1)}, s32[16,64]{1,0:T(8,128)S(1)}, f32[16,3,64]{2,1,0:T(4,128)S(1)}, f32[3,1024]{1,0:T(4,128)S(1)}...) while((s32[]{:T(128)}, f32[16,1,3,64]{3,2,1,0:T(4,128)S(1)}, ...), condition=%wide.region_11.13_spmd.clone, body=%wide.region_10.12_spmd.clone.sunk | while | flops 19859328 | bytes 287865 | solution.py:60
  644.7 0.9 copy.60
  645.6 1.9 bitcast_reduce_fusion
  647.7 74.9 %reduce-scatter.12.cloned.1.call-done = f32[64,3]{1,0:T(8,128)} async-done(((f32[1024,3]{1,0:T(8,128)}), f32[64,3]{1,0:T(8,128)}) %reduce-scatter.12.cloned.1.call-update) | async-done | bytes 784
  722.5 0.9 reshape_bitcast_fusion
  723.5 0.7 fusion.251
  724.2 77.5 %all-reduce.3 = (f32[]{:T(128)}, f32[]{:T(128)}) all-reduce(f32[]{:T(128)} %get-tuple-element.527, f32[]{:T(128)} %fusion.251), channel_id=1, replica_groups=mesh['row'=16,'col'=16] {'row','col'}, use_global_device_ids=true, to_apply=%region_8.10 | all-reduce | flops 2 | bytes 16 | tf_op jit(solution)/shard_map/psum | solution.py:117
  804.0 73.6 %all-reduce.2 = (f32[32]{0:T(128)S(1)}, f32[]{:T(128)}) all-reduce(f32[32]{0:T(128)S(1)} %convolution_bitcast_fusion.25, f32[]{:T(128)} %get-tuple-element.525), channel_id=1, replica_groups=mesh['row'=16,'col'=16] {'row','col'}, use_global_device_ids=true, to_apply=%region_17.19 | all-reduce | flops 33 | bytes 264 | tf_op jit(solution)/shard_map/psum | solution.py:117
  879.3 23.9 %all-gather.5 = f32[16,64,3]{1,2,0:T(4,128)S(1)} all-gather(f32[1,64,3]{1,2,0:T(4,128)S(1)} %bitcast.654), channel_id=3, replica_groups=mesh['row'=16,'col'=16] {'col'}, dimensions={0}, use_global_device_ids=true | all-gather | bytes 13056 | tf_op jit(solution)/shard_map/all_gather | solution.py:126
  903.2 95.1 %while.41 = (s32[]{:T(128)}, f32[16,1,3,64]{3,2,1,0:T(4,128)S(1)}, s32[16,64]{1,0:T(8,128)S(1)}, f32[16,3,64]{2,1,0:T(4,128)S(1)}, f32[3,1024]{1,0:T(4,128)S(1)}...) while((s32[]{:T(128)}, f32[16,1,3,64]{3,2,1,0:T(4,128)S(1)}, ...), condition=%wide.region_19.21_spmd.clone, body=%wide.region_18.20_spmd.clone.sunk | while | flops 19859328 | bytes 287865 | solution.py:60
  998.3 1.0 copy.65
  999.4 74.9 %reduce-scatter.14.cloned.1.call-done = f32[64,3]{1,0:T(8,128)} async-done(((f32[1024,3]{1,0:T(8,128)}), f32[64,3]{1,0:T(8,128)}) %reduce-scatter.14.cloned.1.call-update) | async-done | bytes 784
  1074.3 0.8 copy.63
  1075.9 77.5 %psum.63 = f32[]{:T(128)} all-reduce(f32[]{:T(128)} %fusion.253), channel_id=1, replica_groups=mesh['row'=16,'col'=16] {'row','col'}, use_global_device_ids=true, to_apply=%region_22.24 | all-reduce | flops 1 | bytes 8 | tf_op jit(solution)/shard_map/psum | solution.py:129
  (812 shorter events, 274.4 us)
Async XLA Ops:
  7.2 357.6 %reduce-scatter.10.cloned.1.call-start = ((), (), s32[]{:S(2)}) async-start(), calls=%async_computation.3 | async-start | bytes 557056
  287.2 1.6 copy-start
  287.2 1.6 copy-start.1
  288.7 433.8 %reduce-scatter.12.cloned.1.call-start = ((), (), s32[]{:S(2)}) async-start(), calls=%async_computation.4 | async-start | bytes 557056
  647.6 426.7 %reduce-scatter.14.cloned.1.call-start = ((), (), s32[]{:S(2)}) async-start(), calls=%async_computation.5 | async-start | bytes 557056
Sparse Core Ops, SparseCore 0:
  288.9 75.8 reduce-scatter.9
  647.7 74.7 reduce-scatter.11
  999.5 74.7 reduce-scatter.13
where the time goes:
time: 1160 us
  blocking collectives  595 us (51%)
  matrix products  281 us (24%)
  waiting for transfers between devices  226 us (19%)
  local copies, waits for them, and re-layouts  21.8 us (2%)
  between operations  19.2 us (2%)
  other arithmetic  13.2 us (1%)
    dot_general x432, matrix products, contract(): lax.dot_general(left, right, (((1,), (1,)), ((), ())), precision=highest,...  278 us
    unnamed x6, waiting for transfers between devices  226 us
    psum x3, blocking collectives, residual_stats(): lax.psum((correlation_of(field), jnp.sum(field * field)), ('row', 'col'))  224 us
    all_gather x3, blocking collectives, body(): lax.all_gather(a, 'col', axis=2, tiled=True)  97.6 us
    psum x1, blocking collectives, body(): gram, load = lax.psum((gram_part, load_part), ('row', 'col'))  77.7 us
    psum x1, blocking collectives, body(): curvature = lax.psum(jnp.sum(direction * image), ('row', 'col'))  77.5 us
    unnamed x2, blocking collectives  63.6 us
    all_gather x1, blocking collectives, body(): lax.all_gather(positions, 'col', axis=1, tiled=True)  28.7 us
  transfers between devices with their start and end apart: 3, of which 3 were waited for; matrix products, arithmetic and copies ran while one was open for 0% of the time, Pallas kernels for 0%

commit v1 on v0

--- a/solution.py
+++ b/solution.py
@@ -114,7 +114,7 @@
     residual = rhs - combine(coarse, basis_image)
 
     def residual_stats(field):
-        return lax.psum((correlation_of(field), jnp.sum(field * field)), ("row", "col"))
+        return lax.psum(lax.psum((correlation_of(field), jnp.sum(field * field)), "row"), "col")
 
     correlation, norm_now = residual_stats(residual)
     projection = coarse_solve(correlation)

time: 1160 us -> 1150 us (level)
  blocking collectives: 595 us -> 566 us
  waiting for transfers between devices: 226 us -> 240 us
    psum x3 -> x4, blocking collectives: 224 us -> 118 us  [the longest x2 68.2 us: residual_stats(): lax.psum((correlation_of(field), jnp.sum(field * field)), 'row')]
    psum x1 -> x2, blocking collectives: 77.5 us -> 155 us  [body(): curvature = lax.psum(jnp.sum(direction * image), ('row', 'col'))]
    unnamed x6, waiting for transfers between devices: 226 us -> 240 us
where the time goes in v1:
time: 1150 us
  blocking collectives  566 us (49%)
  matrix products  281 us (24%)
  waiting for transfers between devices  240 us (21%)
  local copies, waits for them, and re-layouts  21.8 us (2%)
  between operations  19.2 us (2%)
  other arithmetic  13.1 us (1%)
    dot_general x432, matrix products, contract(): lax.dot_general(left, right, (((1,), (1,)), ((), ())), precision=highest,...  279 us
    unnamed x6, waiting for transfers between devices  240 us
    psum x2, blocking collectives, body(): curvature = lax.psum(jnp.sum(direction * image), ('row', 'col'))  155 us
    all_gather x3, blocking collectives, body(): lax.all_gather(a, 'col', axis=2, tiled=True)  97.4 us
    psum x1, blocking collectives, body(): gram, load = lax.psum((gram_part, load_part), ('row', 'col'))  77.7 us
    psum x2, blocking collectives, residual_stats(): lax.psum((correlation_of(field), jnp.sum(field * field)), 'row')  68.2 us
    unnamed x2, blocking collectives  63.6 us
    psum x2, blocking collectives, residual_stats(): lax.psum(lax.psum((correlation_of(field), jnp.sum(field * field)), 'row')...  49.9 us
  transfers between devices with their start and end apart: 3, of which 3 were waited for; matrix products, arithmetic and copies ran while one was open for 0% of the time, Pallas kernels for 0%

profile of v1, /device:TPU:1, one launch (start us, length us, event | category | flops | bytes accessed | tf_op | source)
XLA Modules:
  0.0 1147.0 jit_solution(7517966851679531718)
XLA Ops:
  7.2 26.0 %all-gather.2 = f32[16,64,3]{1,2,0:T(4,128)S(1)} all-gather(f32[1,64,3]{1,2,0:T(4,128)} %bitcast.659), channel_id=1, replica_groups=mesh['row'=16,'col'=16] {'row'}, dimensions={0}, use_global_device_ids=true | all-gather | bytes 13056 | tf_op jit(solution)/shard_map/all_gather | solution.py:71
  33.2 28.7 %all-gather.3 = f32[16,64,3]{1,2,0:T(4,128)S(1)} all-gather(f32[1,64,3]{1,2,0:T(4,128)} %bitcast.660), channel_id=1, replica_groups=mesh['row'=16,'col'=16] {'col'}, dimensions={0}, use_global_device_ids=true | all-gather | bytes 13056 | tf_op jit(solution)/shard_map/all_gather | solution.py:75
  61.8 1.3 dynamic-slice
  63.8 0.9 dynamic-update-slice.3
  64.6 39.9 %all-reduce = f32[1024]{0:T(1024)S(1)} all-reduce(f32[1024]{0:T(1024)S(1)} %dynamic-update-slice.3), channel_id=1, replica_groups=mesh['row'=16,'col'=16] {'row'}, use_global_device_ids=true, to_apply=%add | all-reduce | flops 1024 | bytes 8192
  104.6 1.3 dynamic-slice.1
  106.5 0.9 dynamic-update-slice.4
  107.4 23.7 %all-reduce.1 = f32[1024]{0:T(1024)S(1)} all-reduce(f32[1024]{0:T(1024)S(1)} %dynamic-update-slice.4), channel_id=1, replica_groups=mesh['row'=16,'col'=16] {'col'}, use_global_device_ids=true, to_apply=%add.1 | all-reduce | flops 1024 | bytes 8192
  131.4 0.9 copy.39
  132.3 49.4 %all_gather.25 = f32[32,3,1024]{0,1,2:T(4,128)S(1)} all-gather(f32[32,3,64]{0,1,2:T(4,128)S(1)} %copy.39), channel_id=1, replica_groups=mesh['row'=16,'col'=16] {'col'}, dimensions={2}, use_global_device_ids=true | all-gather | bytes 417792 | tf_op jit(solution)/shard_map/all_gather | solution.py:95
  181.7 0.8 copy.41
  182.6 103.7 %while.39 = (s32[]{:T(128)}, f32[16,32,3,64]{3,1,2,0:T(8,128)S(1)}, s32[16,64]{1,0:T(8,128)S(1)}, f32[16,3,64]{2,1,0:T(4,128)S(1)}, f32[3,1024]{1,0:T(4,128)S(1)...) while((s32[]{:T(128)}, f32[16,32,3,64]{3,1,2,0:T(8,128)S(1)}, ...), condition=%wide.region_1.2_spmd.clone, body=%wide.region_0.1_spmd.clone.sunk | while | flops 239297664 | bytes 2417017 | solution.py:60
  183.0 0.7 fusion.370
  185.6 0.7 convolution_add_fusion.10
  189.4 0.7 fusion.370
  192.1 0.7 convolution_add_fusion.10
  195.9 0.7 fusion.370
  198.6 0.7 convolution_add_fusion.10
  202.4 0.7 fusion.370
  205.1 0.7 convolution_add_fusion.10
  208.9 0.7 fusion.370
  215.4 0.7 fusion.370
  218.1 0.7 convolution_add_fusion.10
  221.9 0.7 fusion.370
  228.3 0.7 fusion.370
  231.0 0.7 convolution_add_fusion.10
  234.8 0.7 fusion.370
  237.5 0.7 convolution_add_fusion.10
  241.3 0.7 fusion.370
  244.0 0.7 convolution_add_fusion.10
  247.8 0.7 fusion.370
  254.3 0.7 fusion.370
  256.9 0.7 convolution_add_fusion.10
  260.7 0.7 fusion.370
  267.2 0.7 fusion.370
  269.9 0.7 convolution_add_fusion.10
  273.7 0.7 fusion.370
  276.4 0.7 convolution_add_fusion.10
  280.2 0.7 fusion.370
  286.3 0.9 copy.64
  287.2 1.5 reshape.352
  289.0 75.8 %reduce-scatter.10.cloned.1.call-done = f32[64,96]{1,0:T(8,128)} async-done(((f32[1024,96]{1,0:T(8,128)}), f32[64,96]{1,0:T(8,128)}) %reduce-scatter.10.cloned.1.call-update) | async-done | bytes 24592
  364.9 0.9 reshape.353
  366.0 77.7 %all-reduce.2 = (f32[32,32]{0,1:T(8,128)S(1)}, f32[32]{0:T(128)S(1)}) all-reduce(f32[32,32]{0,1:T(8,128)S(1)} %convolution_bitcast_fusion.18, f32[32]{0:T(128)S(1)} %convolution_bitcast_fusion.27), channel_id=1, replica_groups=mesh['row'=16,'col'=16] {'row','col'}, use_global_device_ids=true, to_apply=%region_3.4 | all-reduce | flops 1056 | bytes 8448 | tf_op jit(solution)/shard_map/psum | solution.py:100
  443.7 2.9 cholesky.18
  448.0 2.4 custom-call.10
  451.7 34.1 %all-reduce.6 = (f32[32]{0:T(128)S(1)}, f32[]{:T(128)}) all-reduce(f32[32]{0:T(128)S(1)} %convolution_bitcast_fusion.26, f32[]{:T(128)} %get-tuple-element.531), channel_id=1, replica_groups=mesh['row'=16,'col'=16] {'row'}, use_global_device_ids=true, to_apply=%region_10.12 | all-reduce | flops 33 | bytes 264 | tf_op jit(solution)/shard_map/psum | solution.py:117
  485.8 24.9 %all-reduce.4 = (f32[32]{0:T(128)S(1)}, f32[]{:T(128)}) all-reduce(f32[32]{0:T(128)S(1)} %get-tuple-element.527, f32[]{:T(128)} %get-tuple-element.528), channel_id=1, replica_groups=mesh['row'=16,'col'=16] {'col'}, use_global_device_ids=true, to_apply=%region_11.13 | all-reduce | flops 33 | bytes 264 | tf_op jit(solution)/shard_map/psum | solution.py:117
  511.1 24.0 %all-gather.4 = f32[16,64,3]{1,2,0:T(4,128)S(1)} all-gather(f32[1,64,3]{1,2,0:T(4,128)S(1)} %bitcast.652), channel_id=2, replica_groups=mesh['row'=16,'col'=16] {'col'}, dimensions={0}, use_global_device_ids=true | all-gather | bytes 13056 | tf_op jit(solution)/shard_map/all_gather | solution.py:126
  535.2 95.2 %while.40 = (s32[]{:T(128)}, f32[16,1,3,64]{3,2,1,0:T(4,128)S(1)}, s32[16,64]{1,0:T(8,128)S(1)}, f32[16,3,64]{2,1,0:T(4,128)S(1)}, f32[3,1024]{1,0:T(4,128)S(1)}...) while((s32[]{:T(128)}, f32[16,1,3,64]{3,2,1,0:T(4,128)S(1)}, ...), condition=%wide.region_13.15_spmd.clone, body=%wide.region_12.14_spmd.clone.sunk | while | flops 19859328 | bytes 287865 | solution.py:60
  630.5 0.9 copy.60
  631.4 1.9 bitcast_reduce_fusion
  633.4 82.0 %reduce-scatter.12.cloned.1.call-done = f32[64,3]{1,0:T(8,128)} async-done(((f32[1024,3]{1,0:T(8,128)}), f32[64,3]{1,0:T(8,128)}) %reduce-scatter.12.cloned.1.call-update) | async-done | bytes 784
  715.4 0.9 reshape_bitcast_fusion
  716.4 0.7 fusion.251
  717.1 77.4 %psum.90 = f32[]{:T(128)} all-reduce(f32[]{:T(128)} %fusion.251), channel_id=1, replica_groups=mesh['row'=16,'col'=16] {'row','col'}, use_global_device_ids=true, to_apply=%region_16.18 | all-reduce | flops 1 | bytes 8 | tf_op jit(solution)/shard_map/psum | solution.py:129
  796.6 34.1 %all-reduce.5 = (f32[32]{0:T(128)S(1)}, f32[]{:T(128)}) all-reduce(f32[32]{0:T(128)S(1)} %convolution_bitcast_fusion.25, f32[]{:T(128)} %get-tuple-element.529), channel_id=1, replica_groups=mesh['row'=16,'col'=16] {'row'}, use_global_device_ids=true, to_apply=%region_20.22 | all-reduce | flops 33 | bytes 264 | tf_op jit(solution)/shard_map/psum | solution.py:117
  830.7 25.0 %all-reduce.3 = (f32[32]{0:T(128)S(1)}, f32[]{:T(128)}) all-reduce(f32[32]{0:T(128)S(1)} %get-tuple-element.525, f32[]{:T(128)} %get-tuple-element.526), channel_id=1, replica_groups=mesh['row'=16,'col'=16] {'col'}, use_global_device_ids=true, to_apply=%region_21.23 | all-reduce | flops 33 | bytes 264 | tf_op jit(solution)/shard_map/psum | solution.py:117
  857.4 24.0 %all-gather.5 = f32[16,64,3]{1,2,0:T(4,128)S(1)} all-gather(f32[1,64,3]{1,2,0:T(4,128)S(1)} %bitcast.654), channel_id=3, replica_groups=mesh['row'=16,'col'=16] {'col'}, dimensions={0}, use_global_device_ids=true | all-gather | bytes 13056 | tf_op jit(solution)/shard_map/all_gather | solution.py:126
  881.5 95.2 %while.41 = (s32[]{:T(128)}, f32[16,1,3,64]{3,2,1,0:T(4,128)S(1)}, s32[16,64]{1,0:T(8,128)S(1)}, f32[16,3,64]{2,1,0:T(4,128)S(1)}, f32[3,1024]{1,0:T(4,128)S(1)}...) while((s32[]{:T(128)}, f32[16,1,3,64]{3,2,1,0:T(4,128)S(1)}, ...), condition=%wide.region_23.25_spmd.clone, body=%wide.region_22.24_spmd.clone.sunk | while | flops 19859328 | bytes 287865 | solution.py:60
  976.6 1.0 copy.65
  977.7 81.8 %reduce-scatter.14.cloned.1.call-done = f32[64,3]{1,0:T(8,128)} async-done(((f32[1024,3]{1,0:T(8,128)}), f32[64,3]{1,0:T(8,128)}) %reduce-scatter.14.cloned.1.call-update) | async-done | bytes 784
  1059.5 0.8 copy.63
  1061.1 77.5 %psum.95 = f32[]{:T(128)} all-reduce(f32[]{:T(128)} %fusion.253), channel_id=1, replica_groups=mesh['row'=16,'col'=16] {'row','col'}, use_global_device_ids=true, to_apply=%region_26.28 | all-reduce | flops 1 | bytes 8 | tf_op jit(solution)/shard_map/psum | solution.py:129
  (814 shorter events, 275.9 us)
Async XLA Ops:
  7.2 357.7 %reduce-scatter.10.cloned.1.call-start = ((), (), s32[]{:S(2)}) async-start(), calls=%async_computation.3 | async-start | bytes 557056
  287.2 1.6 copy-start
  287.2 1.6 copy-start.1
  288.8 426.6 %reduce-scatter.12.cloned.1.call-start = ((), (), s32[]{:S(2)}) async-start(), calls=%async_computation.4 | async-start | bytes 557056
  633.3 426.2 %reduce-scatter.14.cloned.1.call-start = ((), (), s32[]{:S(2)}) async-start(), calls=%async_computation.5 | async-start | bytes 557056
Sparse Core Ops, SparseCore 0:
  288.9 75.8 reduce-scatter.9
  633.4 81.8 reduce-scatter.11
  977.8 81.6 reduce-scatter.13
